TPU v7x, 256 devices: a whole 4x4x8 slice. The times are simulated.
256 devices in a mesh: slab: 64 (over x, y_hi, z), pencil: 4 (over y_lo, core).
Axes of the slice: x: 4, y: 4 (y_hi: 2, y_lo: 2; y = y_hi * 2 + y_lo), z: 8, core: 2. Of those that a mesh axis runs over, the one named last changes fastest.
Arguments:
- fine_blocks: float32 [4, 65536, 3, 256], P('pencil', 'slab'), may hold values from -6 to 6
- owner_slab: int32 [4, 65536, 1], P('pencil', 'slab'), may hold values from 0 to 63; in each aligned block of 1024 rows (0 to 1023, 1024 to 2047, ..., all dimensions but the last counted through in order) at most 32 rows name the same one
- owner_row: int32 [4, 65536], P('pencil', 'slab'), may hold values from 0 to 2047
- valid_counts: int32 [4, 64], P('pencil', 'slab'), may hold values from 768 to 1024
- coarse_field: float32 [3, 256, 256, 1024], P(None, 'slab', 'pencil'), may hold values from -6 to 6
- active: int32 [256, 256, 1024], P('slab', 'pencil'), may hold values 0 or 1
Outputs:
- cleaned: float32 [3, 256, 256, 1024], P(None, 'slab', 'pencil')
Inputs may be any that keep to these rules, and one draw needn't show every extreme that they name: `owner_slab`: among the 1024 blocks of one holder (aligned runs along the second dimension) at most 32 name the same slab, and in some runs a slab is named by exactly 32 of them.
All inputs are finite; a program needn't handle non-finite values. No bound on the sum of `active` on one device may be relied on, other than what follows from the above.
Results may differ from a plain program's by a relative error of at most 0.00005.
Values sent between devices are 32-bit elements; how exact they have to be, the bound alone decides.
No kernel may reach another device: no remote copies, remote signals or barrier semaphores. Data moves between devices by JAX's collectives and lax.ppermute only.
A program may use at most 128 MiB of HBM per device.

v0:
```python
import math

import jax
import jax.numpy as jnp
from jax import lax
from jax.sharding import PartitionSpec as P

SWEEPS = 3


def padded_2(block, sides, width):
    for axis, dim in sides:
        count = lax.axis_size(axis)
        forward = [(i, i + 1) for i in range(count - 1)]
        backward = [(target, source) for source, target in forward]
        low = lax.ppermute(
            lax.slice_in_dim(block, block.shape[dim] - width, None, axis=dim), axis, forward
        )
        high = lax.ppermute(lax.slice_in_dim(block, 0, width, axis=dim), axis, backward)
        block = jnp.concatenate([low, block, high], axis=dim)
    return block


def shifted(value, axis, steps):
    count = lax.axis_size(axis)
    leading, last = (max(0, -steps), min(count, count - steps))
    return lax.ppermute(value, axis, [(source, source + steps) for source in range(leading, last)])


def pair_mean(blocks):
    return (blocks[..., 0::2] + blocks[..., 1::2]) * 0.5


def across_x(padded):
    return jnp.pad(padded[..., 1:], ((0, 0), (0, 0), (0, 1))) + jnp.pad(
        padded[..., :-1], ((0, 0), (0, 0), (1, 0))
    )


def jacobi_sweep(padded, source, inside_mask):
    centre = padded[1:-1, 1:-1]
    beside = padded[2:, 1:-1] + padded[:-2, 1:-1] + padded[1:-1, 2:] + padded[1:-1, :-2]
    beside = beside + across_x(centre)
    return (beside - source) / 6.0 * inside_mask


def extend(potential):
    return padded_2(potential, (("slab", 0), ("pencil", 1)), 1)


def accumulate(target_row, present, arrived, rows_local):
    arrivals = arrived.shape[0]
    flat_rows = arrived.reshape(arrivals, -1)
    step_rows = math.gcd(rows_local, 512)
    live_float = present.astype(jnp.float32)

    def one_block(block_start):
        row_ids = block_start + jnp.arange(step_rows, dtype=jnp.int32)
        selector = jnp.where(target_row[None, :] == row_ids[:, None], live_float[None, :], 0.0)
        summed = jnp.dot(
            selector, flat_rows, precision=lax.Precision.HIGHEST, preferred_element_type=jnp.float32
        )
        return (summed, jnp.sum(selector, axis=1))

    starts = jnp.arange(rows_local // step_rows, dtype=jnp.int32) * step_rows
    summed, counted = lax.map(one_block, starts)
    return (summed.reshape(rows_local, 3, 128), counted.reshape(rows_local))


def shards(fine_blocks, owner_slab, owner_row, valid_counts, coarse_field, active):
    slab_count = lax.axis_size("slab")
    count_held = fine_blocks.shape[1]
    capacity = max(2, 2 * count_held // slab_count)
    depth_z, depth_y, width_x = active.shape
    rows_local = depth_z * depth_y * width_x // 128
    target_slab = owner_slab[0, :, 0]
    block_ids = jnp.arange(count_held, dtype=jnp.int32)
    weights = (block_ids < valid_counts[0, 0]).astype(jnp.float32)
    same_before = (target_slab[None, :] == target_slab[:, None]) & (
        block_ids[None, :] < block_ids[:, None]
    )
    slot_index = target_slab * capacity + jnp.sum(same_before.astype(jnp.int32), axis=1)
    slot_ids = jnp.arange(slab_count * capacity, dtype=jnp.int32)
    matches = slot_index[None, :] == slot_ids[:, None]
    source_block = jnp.sum(jnp.where(matches, block_ids[None, :], 0), axis=1)
    filled = jnp.any(matches, axis=1).astype(jnp.float32)
    row_tags = weights * (owner_row[0].astype(jnp.float32) + 1.0)
    blocks = fine_blocks[0] * weights[:, None, None]
    tag_box = jnp.take(row_tags, source_block, axis=0) * filled
    out_box = jnp.take(blocks, source_block, axis=0) * filled[:, None, None]
    received, labels = (
        lax.all_to_all(out_box, "slab", split_axis=0, concat_axis=0, tiled=True),
        lax.all_to_all(tag_box, "slab", split_axis=0, concat_axis=0, tiled=True),
    )
    arrived = pair_mean(received)
    present = labels > 0.5
    target_row = jnp.where(present, labels - 1.0, 0.0).astype(jnp.int32)
    totals, number = accumulate(target_row, present, arrived, rows_local)
    base = coarse_field.reshape(3, depth_z, depth_y, width_x // 128, 128).transpose(1, 2, 3, 0, 4)
    base = base.reshape(rows_local, 3, 128)
    averaged = totals / jnp.maximum(number, 1.0)[:, None, None]
    restricted = jnp.where((number > 0.5)[:, None, None], averaged, base)
    magnetic = restricted.reshape(depth_z, depth_y, width_x // 128, 3, 128)
    magnetic = magnetic.transpose(3, 0, 1, 2, 4).reshape(3, depth_z, depth_y, width_x)
    face_x, face_y, face_z = (magnetic[0], magnetic[1], magnetic[2])
    above_z = shifted(face_z[:1], "slab", -1)
    above_y = shifted(face_y[:, :1], "pencil", -1)
    next_x = jnp.pad(face_x[:, :, 1:], ((0, 0), (0, 0), (0, 1)))
    next_y = jnp.concatenate([face_y[:, 1:], above_y], axis=1)
    next_z = jnp.concatenate([face_z[1:], above_z], axis=0)
    divergence = next_x - face_x + (next_y - face_y) + (next_z - face_z)
    potential = (0.0 - divergence) / 6.0
    for sweep_index in range(1, SWEEPS):
        potential = jacobi_sweep(extend(potential), divergence, 1.0)
    bordered = extend(potential)
    potential = bordered[1:-1, 1:-1]
    grad_x = potential - jnp.pad(potential[:, :, :-1], ((0, 0), (0, 0), (1, 0)))
    grad_y = potential - bordered[1:-1, :-2]
    grad_z = potential - bordered[:-2, 1:-1]
    cell_mask = active.astype(jnp.float32)
    return jnp.stack(
        [face_x - cell_mask * grad_x, face_y - cell_mask * grad_y, face_z - cell_mask * grad_z]
    )


def solution(mesh):
    in_specs = (
        P("pencil", "slab", None, None),
        P("pencil", "slab", None),
        P("pencil", "slab"),
        P("pencil", "slab"),
        P(None, "slab", "pencil", None),
        P("slab", "pencil", None),
    )
    out_specs = P(None, "slab", "pencil", None)
    return jax.shard_map(shards, mesh=mesh, in_specs=in_specs, out_specs=out_specs, check_vma=False)
```

profile of v0, /device:TPU:3, one launch (start us, length us, event | category | flops | bytes accessed | tf_op | source)
XLA Modules:
  0.0 664.5 jit_solution(680849573534590243)
XLA Ops:
  0.0 1.3 convert_reduce_fusion
  5.4 8.6 %gather_fusion = f32[2048]{0:T(1024)S(1)} fusion(f32[1024]{0:T(1024)S(1)} %fusion.41, s32[2048]{0:T(1024)S(1)} %broadcast_clamp_fusion), kind=kCustom, calls=%fused_computation | custom fusion | bytes 24576 | tf_op jit(solution)/shard_map/jit(_take)/gather | solution.py:89
  14.8 14.1 %all-to-all-start = ((f32[64,32,1]{1,2,0:T(1,128)}), f32[64,32,1]{1,2,0:T(1,128)S(1)}, u32[]{:S(2)}, u32[]{:S(2)}) async-start(f32[64,32,1]{1,2,0:T(1,128)} %bitcast.8), calls=%async_computation | async-start | bytes 65536 | tf_op jit(solution)/shard_map/all_to_all | solution.py:93
  28.9 9.1 %bitcast_multiply_fusion = f32[1024,3,256]{2,1,0:T(4,128)} fusion(f32[1,1024,3,256]{3,1,2,0:T(8,128)S(1)} %copy-done.1, f32[1024]{0:T(1024)S(1)} %fusion.40), kind=kLoop, calls=%fused_computation.18 | loop fusion | flops 786432 | bytes 6295552 | tf_op jit(solution)/shard_map/mul | solution.py:88
  38.0 20.9 %gather_fusion.1 = f32[2048,3,256]{2,1,0:T(4,128)} fusion(f32[1024,3,256]{2,1,0:T(4,128)} %bitcast_multiply_fusion, s32[2048]{0:T(1024)S(1)} %broadcast_clamp_fusion), kind=kCustom, calls=%fused_computation.1 | custom fusion | bytes 12591104 | tf_op jit(solution)/shard_map/jit(_take)/gather | solution.py:90
  58.8 12.0 %select_multiply_fusion = f32[2048,3,256]{2,1,0:T(4,128)} fusion(f32[2048,3,256]{2,1,0:T(4,128)} %gather_fusion.1, f32[2048]{0:T(1024)S(1)} %convert_element_type.51, pred[2048]{0:T(1024)(128)(4,1)S(1)} %compare_and_fusion), kind=kLoop, calls=%fused_computation.14 | loop fusion | flops 3145728 | bytes 12593152 | tf_op jit(solution)/shard_map/mul | solution.py:90
  70.9 12.7 %all-to-all-start.1 = ((f32[2048,3,256]{2,1,0:T(4,128)}), f32[2048,3,256]{2,1,0:T(4,128)}, u32[]{:S(2)}, u32[]{:S(2)}) async-start(f32[2048,3,256]{2,1,0:T(4,128)} %select_multiply_fusion), calls=%async_computation.1 | async-start | bytes 16777216 | tf_op jit(solution)/shard_map/all_to_all | solution.py:92
  83.6 2.4 copy.27
  86.2 181.1 %all-to-all-done.1 = f32[2048,3,256]{2,1,0:T(4,128)} async-done(((f32[2048,3,256]{2,1,0:T(4,128)}), f32[2048,3,256]{2,1,0:T(4,128)}, u32[]{:S(2)}, u32[]{:S(2)}) %all-to-all-start.1) | async-done | bytes 6291488 | tf_op jit(solution)/shard_map/all_to_all | solution.py:92
  267.3 119.0 %slice.129 = f32[2048,3,128]{2,1,0:T(4,128)} slice(f32[2048,3,256]{2,1,0:T(4,128)} %all-to-all-done.1), slice={[0:2048:1], [0:3:1], [0:256:2]} | slice | bytes 6291456 | tf_op jit(solution)/shard_map/slice | solution.py:31
  386.3 119.2 %slice.130 = f32[2048,3,128]{2,1,0:T(4,128)} slice(f32[2048,3,256]{2,1,0:T(4,128)} %all-to-all-done.1), slice={[0:2048:1], [0:3:1], [1:256:2]} | slice | bytes 6291456 | tf_op jit(solution)/shard_map/slice | solution.py:31
  505.5 5.4 add_multiply_fusion
  511.0 3.4 copy.24
  514.4 2.4 copy.25
  516.7 46.5 %while.12 = (s32[]{:T(128)}, f32[4,512,384]{2,1,0:T(8,128)}, f32[4,512]{1,0:T(4,128)S(1)}, s32[2048]{0:T(1024)S(1)}, s32[4]{0:T(128)S(1)}, /*index=5*/f32[2048]{...) while((s32[]{:T(128)}, f32[4,512,384]{2,1,0:T(8,128)}, f32[4,512]{1,0:T(4,128)S(1)}, s32[2048]{0:T(1024)S(1)}, ...), condition=%wide.region_5.6_spmd, body=%wide.region_3.5_spmd.sunk | while | flops 4837081088 | bytes 3977841 | solution.py:66
  518.1 9.7 %fusion.56 = f32[4,512,384]{2,1,0:T(8,128)} fusion(f32[4,512,384]{2,1,0:T(8,128)} %get-tuple-element.155, s32[]{:T(128)} %get-tuple-element.154, f32[2048,384]{1,0:T(8,128)} %get-tuple-element.169, f32[2048]{0:T(1024)S(1)} %get-tuple-element.168, s32[2048]{0:T(1024)S(1)} %get-tuple-element.166, s32[512]{0:T(512)S(1)} %iota_add_fusion.2), kind=kOutput, calls=%fused_computation.11.clone.1 | convolution fusion | flops 4833935360 | bytes 3951104 | tf_op jit(solution)/shard_map/while/body/eval_jaxpr/dot_general | solution.py:60
  529.7 9.7 %fusion.56 = f32[4,512,384]{2,1,0:T(8,128)} fusion(f32[4,512,384]{2,1,0:T(8,128)} %get-tuple-element.155, s32[]{:T(128)} %get-tuple-element.154, f32[2048,384]{1,0:T(8,128)} %get-tuple-element.169, f32[2048]{0:T(1024)S(1)} %get-tuple-element.168, s32[2048]{0:T(1024)S(1)} %get-tuple-element.166, s32[512]{0:T(512)S(1)} %iota_add_fusion.2), kind=kOutput, calls=%fused_computation.11.clone.1 | convolution fusion | flops 4833935360 | bytes 3951104 | tf_op jit(solution)/shard_map/while/body/eval_jaxpr/dot_general | solution.py:60
  541.4 9.6 %fusion.56 = f32[4,512,384]{2,1,0:T(8,128)} fusion(f32[4,512,384]{2,1,0:T(8,128)} %get-tuple-element.155, s32[]{:T(128)} %get-tuple-element.154, f32[2048,384]{1,0:T(8,128)} %get-tuple-element.169, f32[2048]{0:T(1024)S(1)} %get-tuple-element.168, s32[2048]{0:T(1024)S(1)} %get-tuple-element.166, s32[512]{0:T(512)S(1)} %iota_add_fusion.2), kind=kOutput, calls=%fused_computation.11.clone.1 | convolution fusion | flops 4833935360 | bytes 3951104 | tf_op jit(solution)/shard_map/while/body/eval_jaxpr/dot_general | solution.py:60
  553.0 9.7 %fusion.56 = f32[4,512,384]{2,1,0:T(8,128)} fusion(f32[4,512,384]{2,1,0:T(8,128)} %get-tuple-element.155, s32[]{:T(128)} %get-tuple-element.154, f32[2048,384]{1,0:T(8,128)} %get-tuple-element.169, f32[2048]{0:T(1024)S(1)} %get-tuple-element.168, s32[2048]{0:T(1024)S(1)} %get-tuple-element.166, s32[512]{0:T(512)S(1)} %iota_add_fusion.2), kind=kOutput, calls=%fused_computation.11.clone.1 | convolution fusion | flops 4833935360 | bytes 3951104 | tf_op jit(solution)/shard_map/while/body/eval_jaxpr/dot_general | solution.py:60
  563.5 3.2 fusion.16
  567.5 6.1 collective-permute-start.1
  573.6 1.8 fusion.43
  575.3 2.4 squeeze.27
  578.6 5.0 collective-permute-start
  583.6 2.4 slice.174
  587.0 1.5 squeeze.26
  588.4 1.3 slice.172
  589.7 1.4 squeeze.28
  591.1 2.1 slice.137
  593.3 2.5 subtract_multiply_fusion
  595.8 1.9 collective-permute-start.2
  597.8 3.4 collective-permute-start.3
  601.1 4.6 collective-permute-done.2
  605.7 6.4 collective-permute-done.3
  612.2 2.3 collective-permute-start.4
  614.5 3.3 collective-permute-start.5
  619.4 1.9 collective-permute-start.6
  621.3 3.4 collective-permute-start.7
  624.7 4.1 collective-permute-done.6
  628.8 6.4 collective-permute-done.7
  635.3 2.2 collective-permute-start.8
  637.5 3.4 collective-permute-start.9
  642.4 1.9 collective-permute-start.10
  644.3 7.9 %collective-permute-start.11 = (f32[1,64,1024]{2,1,0:T(8,128)S(1)}, f32[1,64,1024]{2,1,0:T(8,128)S(1)}, u32[]{:S(2)}, u32[]{:S(2)}) collective-permute-start(f32[1,64,1024]{2,1,0:T(8,128)S(1)} %get-tuple-element.92), channel_id=1, source_target_pairs={{4,0},{8,4},{12,8},{16,12},{20,16},{24,20},{28,24},{32,28},{36,32}... | collective-permute-start | bytes 786440 | tf_op jit(solution)/shard_map/ppermute | solution.py:19
  652.2 4.0 collective-permute-done.10
  656.2 1.8 collective-permute-done.11
  658.0 2.9 collective-permute-start.12
  662.6 1.9 pad_maximum_fusion
  (72 shorter events, 19.9 us)
Async XLA Ops:
  5.4 23.5 %copy-start.1 = (f32[1,1024,3,256]{3,1,2,0:T(8,128)S(1)}, f32[1,1024,3,256]{3,1,2,0:T(8,128)}, u32[]{:S(2)}) copy-start(f32[1,1024,3,256]{3,1,2,0:T(8,128)} %param.8) | copy-start | bytes 9437188
  14.8 56.1 %all-to-all-start = ((f32[64,32,1]{1,2,0:T(1,128)}), f32[64,32,1]{1,2,0:T(1,128)S(1)}, u32[]{:S(2)}, u32[]{:S(2)}) async-start(f32[64,32,1]{1,2,0:T(1,128)} %bitcast.8), calls=%async_computation | async-start | bytes 65536 | tf_op jit(solution)/shard_map/all_to_all | solution.py:93
  70.9 12.7 %copy-start.2 = (f32[3,4,64,1024]{3,2,1,0:T(8,128)S(1)}, f32[3,4,64,1024]{3,2,1,0:T(8,128)}, u32[]{:S(2)}) copy-start(f32[3,4,64,1024]{3,2,1,0:T(8,128)} %param.12) | copy-start | bytes 9437188
  70.9 196.4 %all-to-all-start.1 = ((f32[2048,3,256]{2,1,0:T(4,128)}), f32[2048,3,256]{2,1,0:T(4,128)}, u32[]{:S(2)}, u32[]{:S(2)}) async-start(f32[2048,3,256]{2,1,0:T(4,128)} %select_multiply_fusion), calls=%async_computation.1 | async-start | bytes 16777216 | tf_op jit(solution)/shard_map/all_to_all | solution.py:92
  567.5 25.8 %collective-permute-start.1 = (f32[1,64,1024]{2,1,0:T(8,128)}, f32[1,64,1024]{2,1,0:T(8,128)S(1)}, u32[]{:S(2)}, u32[]{:S(2)}) collective-permute-start(f32[1,64,1024]{2,1,0:T(8,128)} %slice.139), channel_id=1, source_target_pairs={{4,0},{8,4},{12,8},{16,12},{20,16},{24,20},{28,24},{32,28},{36,32}... | collective-permute-start | bytes 786440 | tf_op jit(solution)/shard_map/ppermute | solution.py:27
  578.6 14.7 %collective-permute-start = (f32[4,1,1024]{2,1,0:T(1,128)S(1)}, f32[4,1,1024]{2,1,0:T(1,128)S(1)}, u32[]{:S(2)}, u32[]{:S(2)}) collective-permute-start(f32[4,1,1024]{2,1,0:T(1,128)S(1)} %slice.175), channel_id=1, source_target_pairs={{1,0},{2,1},{3,2},{5,4},{6,5},{7,6},{9,8},{10,9},{11,10},{13,12},{... | collective-permute-start | bytes 49160 | tf_op jit(solution)/shard_map/ppermute | solution.py:27
  587.0 6.3 copy-start
  595.8 9.9 %collective-permute-start.2 = (f32[1,64,1024]{2,1,0:T(8,128)S(1)}, f32[1,64,1024]{2,1,0:T(8,128)S(1)}, u32[]{:S(2)}, u32[]{:S(2)}) collective-permute-start(f32[1,64,1024]{2,1,0:T(8,128)S(1)} %get-tuple-element.101), channel_id=1, source_target_pairs={{4,0},{8,4},{12,8},{16,12},{20,16},{24,20},{28,24},{32,28},{36,32}... | collective-permute-start | bytes 786440 | tf_op jit(solution)/shard_map/ppermute | solution.py:19
  597.8 14.4 %collective-permute-start.3 = (f32[1,64,1024]{2,1,0:T(8,128)S(1)}, f32[1,64,1024]{2,1,0:T(8,128)S(1)}, u32[]{:S(2)}, u32[]{:S(2)}) collective-permute-start(f32[1,64,1024]{2,1,0:T(8,128)S(1)} %get-tuple-element.100), channel_id=1, source_target_pairs={{0,4},{4,8},{8,12},{12,16},{16,20},{20,24},{24,28},{28,32},{32,36}... | collective-permute-start | bytes 786440 | tf_op jit(solution)/shard_map/ppermute | solution.py:16
  612.2 6.0 collective-permute-start.4
  614.5 4.2 collective-permute-start.5
  619.4 9.4 %collective-permute-start.6 = (f32[1,64,1024]{2,1,0:T(8,128)S(1)}, f32[1,64,1024]{2,1,0:T(8,128)S(1)}, u32[]{:S(2)}, u32[]{:S(2)}) collective-permute-start(f32[1,64,1024]{2,1,0:T(8,128)S(1)} %get-tuple-element.97), channel_id=1, source_target_pairs={{4,0},{8,4},{12,8},{16,12},{20,16},{24,20},{28,24},{32,28},{36,32}... | collective-permute-start | bytes 786440 | tf_op jit(solution)/shard_map/ppermute | solution.py:19
  621.3 14.0 %collective-permute-start.7 = (f32[1,64,1024]{2,1,0:T(8,128)S(1)}, f32[1,64,1024]{2,1,0:T(8,128)S(1)}, u32[]{:S(2)}, u32[]{:S(2)}) collective-permute-start(f32[1,64,1024]{2,1,0:T(8,128)S(1)} %get-tuple-element.96), channel_id=1, source_target_pairs={{0,4},{4,8},{8,12},{12,16},{16,20},{20,24},{24,28},{28,32},{32,36}... | collective-permute-start | bytes 786440 | tf_op jit(solution)/shard_map/ppermute | solution.py:16
  635.3 6.0 collective-permute-start.8
  637.5 4.3 collective-permute-start.9
  641.8 20.0 %copy-start.3 = (s32[4,64,1024]{2,1,0:T(8,128)S(1)}, s32[4,64,1024]{2,1,0:T(8,128)}, u32[]{:S(2)}) copy-start(s32[4,64,1024]{2,1,0:T(8,128)} %param.13) | copy-start | bytes 3145732
  642.4 13.8 %collective-permute-start.10 = (f32[1,64,1024]{2,1,0:T(8,128)S(1)}, f32[1,64,1024]{2,1,0:T(8,128)S(1)}, u32[]{:S(2)}, u32[]{:S(2)}) collective-permute-start(f32[1,64,1024]{2,1,0:T(8,128)S(1)} %get-tuple-element.93), channel_id=1, source_target_pairs={{0,4},{4,8},{8,12},{12,16},{16,20},{20,24},{24,28},{28,32},{32,36}... | collective-permute-start | bytes 786440 | tf_op jit(solution)/shard_map/ppermute | solution.py:16
  644.3 13.7 %collective-permute-start.11 = (f32[1,64,1024]{2,1,0:T(8,128)S(1)}, f32[1,64,1024]{2,1,0:T(8,128)S(1)}, u32[]{:S(2)}, u32[]{:S(2)}) collective-permute-start(f32[1,64,1024]{2,1,0:T(8,128)S(1)} %get-tuple-element.92), channel_id=1, source_target_pairs={{4,0},{8,4},{12,8},{16,12},{20,16},{24,20},{28,24},{32,28},{36,32}... | collective-permute-start | bytes 786440 | tf_op jit(solution)/shard_map/ppermute | solution.py:19
  658.0 3.8 collective-permute-start.12
where the time goes:
time: 666 us; the launch traced here: 664 us
  local copies, waits for them, and re-layouts  296 us (44%)
  waiting for transfers between devices  211 us (32%)
  starting transfers between devices  72.2 us (11%)
  other arithmetic  46.4 us (7%)
  matrix products  38.6 us (6%)
    slice x2, local copies, waits for them, and re-layouts, pair_mean(): return (blocks[..., 0::2] + blocks[..., 1::2]) * 0.5  238 us
    all_to_all x1, waiting for transfers between devices, shards(): lax.all_to_all(out_box, 'slab', split_axis=0, concat_axis=0, tiled=True)  181 us
    dot_general x4, matrix products, one_block(): jnp.dot(selector, flat_rows, precision=lax.Precision.HIGHEST, preferred_e...  38.6 us
    gather x1, local copies, waits for them, and re-layouts, shards(): out_box = jnp.take(blocks, source_block, axis=0) * filled[:, None, None]  20.9 us
    ppermute x6, waiting for transfers between devices, padded_2(): lax.ppermute(lax.slice_in_dim(block, block.shape[dim] - width, None, axis...  18.9 us
    ppermute x6, starting transfers between devices, padded_2(): lax.ppermute(lax.slice_in_dim(block, block.shape[dim] - width, None, axis...  18.1 us
    ppermute x5, starting transfers between devices, padded_2(): lax.ppermute(lax.slice_in_dim(block, 0, width, axis=dim), axis, backward)  16.2 us
    all_to_all x1, starting transfers between devices, shards(): lax.all_to_all(tag_box, 'slab', split_axis=0, concat_axis=0, tiled=True)  14.1 us
  transfers between devices with their start and end apart: 15, of which 10 were waited for; matrix products, arithmetic and copies ran while one was open for 9% of the time, Pallas kernels for 0%

commit v1 on v0

v1 whole, which is shorter than its diff:
```python
import functools

import jax
import jax.numpy as jnp
from jax import lax
from jax.experimental import pallas as pl
from jax.experimental.pallas import tpu as pltpu
from jax.sharding import PartitionSpec as P

F32, BF16 = jnp.float32, jnp.bfloat16
LANES = 128
SLOTS = 32
TAG_ROW = 3 * SLOTS
BOX_ROWS = TAG_ROW + 8
VMEM_BYTES = 48 << 20


def iota(shape, dim):
    return lax.broadcasted_iota(jnp.int32, shape, dim)


def halves(value):
    high = value.astype(BF16)
    return high, (value - high.astype(F32)).astype(BF16)


def dot(left, right):
    return jnp.dot(left, right, preferred_element_type=F32)


def dot_rows(left, right):
    return lax.dot_general(left, right, (((1,), (1,)), ((), ())), preferred_element_type=F32)


def hot(mask):
    return jnp.where(mask, 1.0, 0.0)


def pack_kernel(info, slab, row, fine, box, coarse, slots, tags):
    count_held = slab.shape[1]
    slab_count = tags.shape[0]
    group = box.shape[0]
    step = pl.program_id(0)

    @pl.when(step == 0)
    def _():
        valid = info[0]
        lane_base = info[1]
        width = 3 * LANES
        chunk = min(256, count_held)
        pick = jnp.where(
            iota((2 * LANES, LANES), 0) // 2 == iota((2 * LANES, LANES), 1), 0.5, 0.0
        ).astype(BF16)
        for part in range(3):
            for start in range(0, count_held, chunk):
                rows = slice(start, start + chunk)
                high, low = halves(fine[part, rows, :])
                mean_high, mean_low = halves(dot(high, pick) + dot(low, pick))
                coarse[rows, part * LANES : (part + 1) * LANES] = mean_high
                coarse[rows, width + part * LANES : width + (part + 1) * LANES] = mean_low
        piece = min(LANES, count_held)
        before = hot(iota((piece, piece), 0) < iota((piece, piece), 1)).astype(BF16)
        ones = jnp.ones((piece, piece), BF16)
        running = jnp.zeros((slab_count, piece), F32)
        table = jnp.zeros((slab_count, LANES), F32)
        for start in range(0, count_held, piece):
            lanes = slice(start, start + piece)
            live = iota((1, piece), 1) + start < valid
            target = jnp.where(live, slab[:, lanes], -1)
            named = hot(iota((slab_count, piece), 0) == target)
            named16 = named.astype(BF16)
            earlier = dot(named16, before) + running
            running = running + dot(named16, ones)
            rank = jnp.sum(named * earlier, axis=0, keepdims=True).astype(jnp.int32)
            slots[:, lanes] = jnp.where(live, target * SLOTS + rank, -1)
            tag = row[:, lanes] + 1
            place = hot(iota((LANES, piece), 0) == rank + lane_base).astype(BF16)
            upper = (named * (tag // 64).astype(F32)).astype(BF16)
            lower = (named * (tag % 64).astype(F32)).astype(BF16)
            table = table + dot_rows(upper, place) * 64.0 + dot_rows(lower, place)
        tags[...] = table

    wanted = iota((group * SLOTS, 1), 0) + step * (group * SLOTS)
    chosen = hot(slots[...] == wanted).astype(BF16)
    both = dot(chosen, coarse[...])
    for part in range(3):
        lanes = slice(part * LANES, (part + 1) * LANES)
        low_lanes = slice((3 + part) * LANES, (4 + part) * LANES)
        rows = (both[:, lanes] + both[:, low_lanes]).reshape(group, SLOTS, LANES)
        box[:, part * SLOTS : (part + 1) * SLOTS, :] = rows
    mine = tags[pl.ds(pl.multiple_of(step * group, group), group), :]
    box[:, TAG_ROW:, :] = jnp.broadcast_to(mine[:, None, :], (group, 8, LANES))


def pack(info, slab, row, fine, slab_count):
    count_held = slab.shape[1]
    group = min(8, slab_count)
    whole = lambda *dims: pl.BlockSpec(dims, lambda i: (0,) * len(dims))
    return pl.pallas_call(
        pack_kernel,
        grid=(slab_count // group,),
        in_specs=[
            pl.BlockSpec(memory_space=pltpu.SMEM),
            whole(1, count_held),
            whole(1, count_held),
            whole(3, count_held, 2 * LANES),
        ],
        out_specs=pl.BlockSpec((group, BOX_ROWS, LANES), lambda i: (i, 0, 0)),
        out_shape=jax.ShapeDtypeStruct((slab_count, BOX_ROWS, LANES), F32),
        scratch_shapes=[
            pltpu.VMEM((count_held, 6 * LANES), BF16),
            pltpu.VMEM((1, count_held), jnp.int32),
            pltpu.VMEM((slab_count, LANES), F32),
        ],
        compiler_params=pltpu.CompilerParams(vmem_limit_bytes=VMEM_BYTES),
        name="pack",
    )(info, slab, row, fine)


def accumulate_kernel(
    box, base, field, partial, low_planes, high_planes, low_rows, high_rows, rows16, tags, above
):
    slab_count = box.shape[0]
    step = pl.program_id(0)
    last = pl.num_programs(0) - 1
    plane = last - step
    depth_y, width_x = base.shape[2], base.shape[3]
    tile_rows = depth_y * (width_x // LANES)
    width = 3 * LANES

    @pl.when(step == 0)
    def _():
        tags[...] = jnp.sum(box[:, TAG_ROW, :].reshape(slab_count // 4, 4, LANES), axis=1)
        chunk = min(8, slab_count)
        for part in range(3):
            for start in range(0, slab_count, chunk):
                value = box[start : start + chunk, part * SLOTS : (part + 1) * SLOTS, :]
                high, low = halves(value.reshape(chunk * SLOTS, LANES))
                rows = slice(start * SLOTS, (start + chunk) * SLOTS)
                rows16[rows, part * LANES : (part + 1) * LANES] = high
                rows16[rows, width + part * LANES : width + (part + 1) * LANES] = low
        above[...] = jnp.zeros_like(above)

    index = iota((tile_rows, 1), 0)
    y = index // 64 * 8 + index % 8
    row_tag = (plane * tile_rows + y * 8 + index // 8 % 8 + 1).astype(F32)
    masks = [hot(tags[g : g + 1, :] == row_tag) for g in range(slab_count // 4)]
    counted = functools.reduce(lambda a, b: a + b, masks).astype(BF16)
    number = dot(counted, jnp.ones((LANES, LANES), BF16))
    chosen = jnp.concatenate([mask.astype(BF16) for mask in masks], axis=1)
    both = dot(chosen, rows16[...])
    some = number > 0.5
    scale = 1.0 / jnp.maximum(number, 1.0)
    for part in range(3):
        totals = both[:, part * LANES : (part + 1) * LANES]
        totals = totals + both[:, (3 + part) * LANES : (4 + part) * LANES]
        averaged = totals * scale
        for y8 in range(depth_y // 8):
            for xb in range(width_x // LANES):
                at = slice(y8 * 64 + xb * 8, y8 * 64 + xb * 8 + 8)
                ys, xs = slice(y8 * 8, y8 * 8 + 8), slice(xb * LANES, (xb + 1) * LANES)
                field[part, 0, ys, xs] = jnp.where(some[at], averaged[at], base[part, 0, ys, xs])

    edge_x = iota((8, width_x), 1) == width_x - 1
    last_y = iota((8, width_x), 0) == 7
    for y8 in range(depth_y // 8):
        ys = slice(y8 * 8, y8 * 8 + 8)
        face_x, face_y, face_z = (field[part, 0, ys, :] for part in range(3))
        next_x = jnp.where(edge_x, 0.0, pltpu.roll(face_x, width_x - 1, 1))
        after = field[1, 0, y8 * 8 + 8 : y8 * 8 + 9, :] if y8 * 8 + 8 < depth_y else 0.0
        next_y = jnp.where(last_y, after, pltpu.roll(face_y, 7, 0))
        value = (next_x - face_x) + (next_y - face_y) + (above[ys, :] - face_z)
        partial[0, ys, :] = value
        above[ys, :] = face_z

        @pl.when(step < last)
        def _():
            low_planes[plane - 1, ys, :] = value

        @pl.when(plane < 2)
        def _():
            high_planes[plane, ys, :] = value

        @pl.when(plane == 0)
        def _():
            high_planes[2, ys, :] = face_z

    low_rows[plane] = partial[0, depth_y - 8 :, :]
    face_row = field[1, 0, 0:1, :]
    high_rows[plane] = jnp.where(iota((8, width_x), 0) == 2, face_row, partial[0, 0:8, :])

    @pl.when(plane == 0)
    def _():
        low_rows[last + 1] = field[2, 0, depth_y - 8 :, :]
        high_rows[last + 1] = field[2, 0, 0:8, :]


def accumulate(box, base):
    slab_count = box.shape[0]
    _, depth_z, depth_y, width_x = base.shape
    top = depth_z - 1
    whole = lambda *dims: pl.BlockSpec(dims, lambda i: (0,) * len(dims))
    planes = pl.BlockSpec((3, 1, depth_y, width_x), lambda i: (0, top - i, 0, 0))
    shape = lambda *dims: jax.ShapeDtypeStruct(dims, F32)
    return pl.pallas_call(
        accumulate_kernel,
        grid=(depth_z,),
        in_specs=[whole(*box.shape), planes],
        out_specs=[
            planes,
            pl.BlockSpec((1, depth_y, width_x), lambda i: (top - i, 0, 0)),
            whole(3, depth_y, width_x),
            whole(3, depth_y, width_x),
            whole(depth_z + 1, 8, width_x),
            whole(depth_z + 1, 8, width_x),
        ],
        out_shape=[
            shape(*base.shape),
            shape(depth_z, depth_y, width_x),
            shape(3, depth_y, width_x),
            shape(3, depth_y, width_x),
            shape(depth_z + 1, 8, width_x),
            shape(depth_z + 1, 8, width_x),
        ],
        scratch_shapes=[
            pltpu.VMEM((slab_count * SLOTS, 6 * LANES), BF16),
            pltpu.VMEM((slab_count // 4, LANES), F32),
            pltpu.VMEM((depth_y, width_x), F32),
        ],
        compiler_params=pltpu.CompilerParams(vmem_limit_bytes=VMEM_BYTES),
        name="accumulate",
    )(box, base)


def corner_kernel(below, above, own, beside, low_corner, high_corner):
    planes, _, width_x = below.shape
    line = iota((8, width_x), 0)
    for z in range(planes):
        value = below[z]
        if z < planes - 1:
            value = value + jnp.where(line == 7, own[z, 2:3, :], 0.0)
        value = jnp.where(line > 4, value, above[z])
        beside[z] = value
        if 1 <= z < planes - 1:
            low_corner[z - 1] = value
        if z < 2:
            high_corner[z] = value
        if z == planes - 1:
            high_corner[2] = value


def corners(below, above, own):
    shape = lambda *dims: jax.ShapeDtypeStruct(dims, F32)
    planes, _, width_x = below.shape
    return pl.pallas_call(
        corner_kernel,
        out_shape=[shape(*below.shape), shape(3, 8, width_x), shape(3, 8, width_x)],
        name="corners",
    )(below, above, own)


def correct_kernel(
    flags, field, partial, below, above, beside, below_beside, above_beside, active, out, first, second, third
):
    depth_z, depth_y, width_x = partial.shape
    planes = depth_z + 5
    tiles = depth_y // 8 + 2
    line = iota((8, width_x), 0)
    column = iota((8, width_x), 1)
    has_low_z, has_high_z, has_low_y, has_high_y = (flags[i] for i in range(4))
    sixth = 1.0 / 6.0

    def z_scale(p):
        return has_low_z if p < 3 else (has_high_z if p >= depth_z + 3 else 1.0)

    def y_scale(t):
        return has_low_y if t == 0 else (has_high_y if t == tiles - 1 else 1.0)

    for p in range(planes):
        z = p - 3
        for t in range(tiles):
            ys = slice(t * 8 - 8, t * 8)
            inner = 0 < t < tiles - 1
            if z < 0:
                value = below[p, ys, :] if inner else below_beside[p]
                edge = below_beside[p, 2:3, :]
                if z == -1:
                    value = value + (field[2, 0, ys, :] if inner else beside[depth_z])
            elif z < depth_z:
                value = partial[z, ys, :] if inner else beside[z]
                edge = beside[z, 2:3, :]
                if z == depth_z - 1:
                    value = value + (above[2, ys, :] if inner else above_beside[2])
            else:
                value = above[z - depth_z, ys, :] if inner else above_beside[z - depth_z]
                edge = above_beside[z - depth_z, 2:3, :]
            if t == tiles - 2:
                value = value + jnp.where(line == 7, edge, 0.0)
            first[p, t * 8 : t * 8 + 8, :] = value * (-sixth * z_scale(p) * y_scale(t))

    def around(source, p, t):
        centre = source[p, t * 8 : t * 8 + 8, :]
        total = source[p - 1, t * 8 : t * 8 + 8, :] + source[p + 1, t * 8 : t * 8 + 8, :]
        lower = source[p, t * 8 - 1 : t * 8, :] if t > 0 else 0.0
        upper = source[p, t * 8 + 8 : t * 8 + 9, :] if t < tiles - 1 else 0.0
        total = total + jnp.where(line == 0, lower, pltpu.roll(centre, 1, 0))
        total = total + jnp.where(line == 7, upper, pltpu.roll(centre, 7, 0))
        total = total + jnp.where(column == 0, 0.0, pltpu.roll(centre, 1, 1))
        return total + jnp.where(column == width_x - 1, 0.0, pltpu.roll(centre, width_x - 1, 1))

    for p in range(1, planes - 1):
        for t in range(tiles):
            value = around(first, p, t) * sixth + first[p, t * 8 : t * 8 + 8, :]
            scaled = not (3 <= p < depth_z + 3 and 0 < t < tiles - 1)
            second[p, t * 8 : t * 8 + 8, :] = value * (z_scale(p) * y_scale(t)) if scaled else value
    for p in range(2, depth_z + 3):
        for t in range(tiles - 1):
            value = around(second, p, t) * sixth + first[p, t * 8 : t * 8 + 8, :]
            scaled = not (3 <= p and 0 < t)
            third[p, t * 8 : t * 8 + 8, :] = value * (z_scale(p) * y_scale(t)) if scaled else value
    for z in range(depth_z):
        p = z + 3
        for t in range(1, tiles - 1):
            ys, rows = slice(t * 8 - 8, t * 8), slice(t * 8, t * 8 + 8)
            mask = active[z, ys, :].astype(F32)
            centre = third[p, rows, :]
            left = jnp.where(column == 0, 0.0, pltpu.roll(centre, 1, 1))
            lower = jnp.where(line == 0, third[p, t * 8 - 1 : t * 8, :], pltpu.roll(centre, 1, 0))
            under = third[p - 1, rows, :]
            for part, other in enumerate((left, lower, under)):
                out[part, z, ys, :] = field[part, z, ys, :] - mask * (centre - other)


def correct(flags, field, partial, below, above, beside, below_beside, above_beside, active):
    depth_z, depth_y, width_x = partial.shape
    extended = pltpu.VMEM((depth_z + 5, depth_y + 16, width_x), F32)
    vmem = pl.BlockSpec(memory_space=pltpu.VMEM)
    return pl.pallas_call(
        correct_kernel,
        in_specs=[pl.BlockSpec(memory_space=pltpu.SMEM)] + [vmem] * 8,
        out_specs=vmem,
        out_shape=jax.ShapeDtypeStruct(field.shape, F32),
        scratch_shapes=[extended] * 3,
        compiler_params=pltpu.CompilerParams(vmem_limit_bytes=VMEM_BYTES),
        name="correct",
    )(flags, field, partial, below, above, beside, below_beside, above_beside, active)


def moved(value, axis, steps):
    count = lax.axis_size(axis)
    pairs = [(i, i + steps) for i in range(count) if 0 <= i + steps < count]
    return lax.ppermute(value, axis, pairs)


def shards(fine_blocks, owner_slab, owner_row, valid_counts, coarse_field, active):
    slab_count, band_count = lax.axis_size("slab"), lax.axis_size("pencil")
    slab_at, band_at = lax.axis_index("slab"), lax.axis_index("pencil")
    count_held = fine_blocks.shape[1]
    info = jnp.stack([valid_counts[0, 0], slab_at % 4 * SLOTS])
    fine = fine_blocks[0].transpose(1, 0, 2)
    out_box = pack(info, owner_slab.reshape(1, count_held), owner_row, fine, slab_count)
    box = lax.all_to_all(out_box, "slab", split_axis=0, concat_axis=0, tiled=True)
    field, partial, low_planes, high_planes, low_rows, high_rows = accumulate(box, coarse_field)
    rows_below = moved(low_rows, "pencil", 1)
    rows_above = moved(high_rows, "pencil", -1)
    below = moved(low_planes, "slab", 1)
    above = moved(high_planes, "slab", -1)
    beside, low_corner, high_corner = corners(rows_below, rows_above, high_rows)
    below_beside = moved(low_corner, "slab", 1)
    above_beside = moved(high_corner, "slab", -1)
    flags = jnp.stack(
        [slab_at > 0, slab_at < slab_count - 1, band_at > 0, band_at < band_count - 1]
    ).astype(F32)
    return correct(flags, field, partial, below, above, beside, below_beside, above_beside, active)


def solution(mesh):
    in_specs = (
        P("pencil", "slab", None, None),
        P("pencil", "slab", None),
        P("pencil", "slab"),
        P("pencil", "slab"),
        P(None, "slab", "pencil", None),
        P("slab", "pencil", None),
    )
    out_specs = P(None, "slab", "pencil", None)
    return jax.shard_map(shards, mesh=mesh, in_specs=in_specs, out_specs=out_specs, check_vma=False)
```

time: 666 us -> 175 us (0.26)
  local copies, waits for them, and re-layouts: 296 us -> 6.52 us
  waiting for transfers between devices: 211 us -> 9.68 us
  blocking collectives: 0 us -> 91.3 us
  other arithmetic: 46.4 us -> 0.16 us
  starting transfers between devices: 72.2 us -> 30.1 us
  matrix products: 38.6 us -> 0 us
  Pallas kernels: 0 us -> 34.6 us
    slice x15 -> x0, local copies, waits for them, and re-layouts: 249 us -> none  [the longest x2 238 us: pair_mean(): return (blocks[..., 0::2] + blocks[..., 1::2]) * 0.5]
    all_to_all x2 -> x0, waiting for transfers between devices: 181 us -> none  [the longest x1 181 us: shards(): lax.all_to_all(out_box, 'slab', split_axis=0, concat_axis=0, tiled=True)]
    all_to_all x0 -> x1, blocking collectives: none -> 91.3 us  [shards(): lax.all_to_all(out_box, 'slab', split_axis=0, concat_axis=0, tiled=True)]
    dot_general x4 -> x0, matrix products: 38.6 us -> none  [one_block(): jnp.dot(selector, flat_rows, precision=lax.Precision.HIGHEST, preferred_e...]
    pallas_call x0 -> x4, Pallas kernels: none -> 34.6 us  [the longest x1 17 us: accumulate(): pl.pallas_call(accumulate_kernel, grid=(depth_z,), in_specs=[whole(*box.s...]
    gather x3 -> x0, local copies, waits for them, and re-layouts: 29.5 us -> none  [the longest x1 20.9 us: shards(): out_box = jnp.take(blocks, source_block, axis=0) * filled[:, None, None]]
    mul x6 -> x0, other arithmetic: 27.2 us -> none  [the longest x1 12 us: shards(): out_box = jnp.take(blocks, source_block, axis=0) * filled[:, None, None]]
    all_to_all x2 -> x0, starting transfers between devices: 26.8 us -> none  [the longest x1 14.1 us: shards(): lax.all_to_all(tag_box, 'slab', split_axis=0, concat_axis=0, tiled=True)]
  transfers between devices with their start and end apart: 15 -> 6, of which waited for: 10 -> 4; matrix products, arithmetic and copies ran while one was open for 9% -> 0% of each run, Pallas kernels for 0% -> 1%
where the time goes in v1:
time: 175 us; the launch traced here: 173 us
  blocking collectives  91.3 us (52%)
  Pallas kernels  34.6 us (20%)
  starting transfers between devices  30.1 us (17%)
  waiting for transfers between devices  9.68 us (6%)
  local copies, waits for them, and re-layouts  6.52 us (4%)
    all_to_all x1, blocking collectives, shards(): lax.all_to_all(out_box, 'slab', split_axis=0, concat_axis=0, tiled=True)  91.3 us
    ppermute x6, starting transfers between devices, moved(): return lax.ppermute(value, axis, pairs)  30.1 us
    pallas_call x1, Pallas kernels, accumulate(): pl.pallas_call(accumulate_kernel, grid=(depth_z,), in_specs=[whole(*box.s...  17 us
    ppermute x6, waiting for transfers between devices, moved(): return lax.ppermute(value, axis, pairs)  9.68 us
    pallas_call x1, Pallas kernels, pack(): pl.pallas_call(pack_kernel, grid=(slab_count // group,), in_specs=[pl.Blo...  9.13 us
    pallas_call x1, Pallas kernels, correct(): pl.pallas_call(correct_kernel, in_specs=[pl.BlockSpec(memory_space=pltpu....  6.66 us
    unnamed x18, local copies, waits for them, and re-layouts  6.52 us
  transfers between devices with their start and end apart: 6, of which 4 were waited for; matrix products, arithmetic and copies ran while one was open for 0% of the time, Pallas kernels for 1%

profile of v1, /device:TPU:3, one launch (start us, length us, event | category | flops | bytes accessed | tf_op | source)
XLA Modules:
  0.0 173.1 jit_solution(14729186271937688497)
XLA Ops:
  0.7 0.1 pad_add_fusion.info
  0.7 0.0 copy-start
  0.7 1.9 %copy-done = f32[1,1024,3,256]{3,1,2,0:T(8,128)S(1)} copy-done((f32[1,1024,3,256]{3,1,2,0:T(8,128)S(1)}, f32[1,1024,3,256]{3,1,2,0:T(8,128)}, u32[]{:S(2)}) %copy-start) | copy-done | bytes 3145752
  2.6 0.0 copy-start.5
  2.6 0.7 copy-done.5
  3.3 0.0 copy-start.6
  3.3 0.7 copy-done.6
  4.0 9.1 %pack.1 = f32[64,104,128]{2,1,0:T(8,128)} custom-call(s32[2]{0:T(128)S(1)} %pad_add_fusion.info, s32[1,1024]{1,0:T(1,128)S(1)} %bitcast.12, s32[1,1024]{1,0:T(1,128)S(1)} %copy-done.6, f32[3,1024,256]{2,1,0:T(8,128)S(1)} %bitcast.11), custom_call_target="tpu_custom_call" | custom-call | tf_op jit(solution)/shard_map/pack/pallas_call | solution.py:99
  13.1 91.3 %all_to_all.5.box = f32[64,104,128]{2,1,0:T(8,128)} all-to-all(f32[64,104,128]{2,1,0:T(8,128)} %pack.1), channel_id=1, replica_groups=mesh['slab'=64,'pencil'=4] {'slab'}, dimensions={0} | all-to-all | bytes 6815744 | tf_op jit(solution)/shard_map/all_to_all | solution.py:362
  104.4 0.0 copy-start.2
  104.4 17.0 %accumulate.1 = (f32[3,4,64,1024]{3,2,1,0:T(8,128)S(1)}, f32[4,64,1024]{2,1,0:T(8,128)S(1)}, f32[3,64,1024]{2,1,0:T(8,128)}, f32[3,64,1024]{2,1,0:T(8,128)}, f32...) custom-call(f32[64,104,128]{2,1,0:T(8,128)} %all_to_all.5.box, f32[3,4,64,1024]{3,2,1,0:T(8,128)} %base.1), custom_call_target="tpu_custom_call" | custom-call | tf_op jit(solution)/shard_map/accumulate/pallas_call | solution.py:205
  121.4 0.0 copy-start.1
  121.4 1.7 copy-done.1
  123.0 0.0 copy-start.3
  123.0 3.9 %collective-permute-start = (f32[3,64,1024]{2,1,0:T(8,128)}, f32[3,64,1024]{2,1,0:T(8,128)S(1)}, u32[]{:S(2)}, u32[]{:S(2)}) collective-permute-start(f32[3,64,1024]{2,1,0:T(8,128)} %get-tuple-element.16), channel_id=1, source_target_pairs={{0,4},{4,8},{8,12},{12,16},{16,20},{20,24},{24,28},{28,32},{32,36}... | collective-permute-start | bytes 2359304 | tf_op jit(solution)/shard_map/ppermute | solution.py:352
  126.9 5.9 %collective-permute-start.1 = (f32[3,64,1024]{2,1,0:T(8,128)}, f32[3,64,1024]{2,1,0:T(8,128)}, u32[]{:S(2)}, u32[]{:S(2)}) collective-permute-start(f32[3,64,1024]{2,1,0:T(8,128)} %get-tuple-element.17), channel_id=1, source_target_pairs={{4,0},{8,4},{12,8},{16,12},{20,16},{24,20},{28,24},{32,28},{36,32}... | collective-permute-start | bytes 2359304 | tf_op jit(solution)/shard_map/ppermute | solution.py:352
  132.8 7.1 %collective-permute-start.2 = (f32[5,8,1024]{2,1,0:T(8,128)S(1)}, f32[5,8,1024]{2,1,0:T(8,128)S(1)}, u32[]{:S(2)}, u32[]{:S(2)}) collective-permute-start(f32[5,8,1024]{2,1,0:T(8,128)S(1)} %get-tuple-element.18), channel_id=1, source_target_pairs={{0,1},{1,2},{2,3},{4,5},{5,6},{6,7},{8,9},{9,10},{10,11},{12,13},{... | collective-permute-start | bytes 491528 | tf_op jit(solution)/shard_map/ppermute | solution.py:352
  139.9 1.9 %collective-permute-start.3 = (f32[5,8,1024]{2,1,0:T(8,128)S(1)}, f32[5,8,1024]{2,1,0:T(8,128)S(1)}, u32[]{:S(2)}, u32[]{:S(2)}) collective-permute-start(f32[5,8,1024]{2,1,0:T(8,128)S(1)} %get-tuple-element.19.own), channel_id=1, source_target_pairs={{1,0},{2,1},{3,2},{5,4},{6,5},{7,6},{9,8},{10,9},{11,10},{13,12},{... | collective-permute-start | bytes 491528 | tf_op jit(solution)/shard_map/ppermute | solution.py:352
  141.9 7.0 %collective-permute-done.2.below = f32[5,8,1024]{2,1,0:T(8,128)S(1)} collective-permute-done((f32[5,8,1024]{2,1,0:T(8,128)S(1)}, f32[5,8,1024]{2,1,0:T(8,128)S(1)}, u32[]{:S(2)}, u32[]{:S(2)}) %collective-permute-start.2) | collective-permute-done | bytes 163872 | tf_op jit(solution)/shard_map/ppermute | solution.py:352
  148.8 0.0 copy-start.7
  148.8 0.8 collective-permute-done.3.above
  149.7 0.0 copy-done.3
  149.7 0.0 copy-done.7
  149.7 0.0 copy-start.8
  149.7 0.7 copy-done.8
  150.4 1.8 %corners.1 = (f32[5,8,1024]{2,1,0:T(8,128)}, f32[3,8,1024]{2,1,0:T(8,128)}, f32[3,8,1024]{2,1,0:T(8,128)}) custom-call(f32[5,8,1024]{2,1,0:T(8,128)} %copy-done.7, f32[5,8,1024]{2,1,0:T(8,128)} %copy-done.8, f32[5,8,1024]{2,1,0:T(8,128)} %copy-done.3), custom_call_target="tpu_custom_call" | custom-call | tf_op jit(solution)/shard_map/corners/pallas_call | solution.py:255
  152.2 1.9 %collective-permute-start.4 = (f32[3,8,1024]{2,1,0:T(8,128)}, f32[3,8,1024]{2,1,0:T(8,128)S(1)}, u32[]{:S(2)}, u32[]{:S(2)}) collective-permute-start(f32[3,8,1024]{2,1,0:T(8,128)} %get-tuple-element.21), channel_id=1, source_target_pairs={{0,4},{4,8},{8,12},{12,16},{16,20},{20,24},{24,28},{28,32},{32,36}... | collective-permute-start | bytes 294920 | tf_op jit(solution)/shard_map/ppermute | solution.py:352
  154.1 9.4 %collective-permute-start.5 = (f32[3,8,1024]{2,1,0:T(8,128)}, f32[3,8,1024]{2,1,0:T(8,128)S(1)}, u32[]{:S(2)}, u32[]{:S(2)}) collective-permute-start(f32[3,8,1024]{2,1,0:T(8,128)} %get-tuple-element.22), channel_id=1, source_target_pairs={{4,0},{8,4},{12,8},{16,12},{20,16},{24,20},{28,24},{32,28},{36,32}... | collective-permute-start | bytes 294920 | tf_op jit(solution)/shard_map/ppermute | solution.py:352
  163.6 0.1 add_convert_fusion.flags
  163.6 0.2 collective-permute-done.4.below_beside
  163.8 1.7 collective-permute-done.5.above_beside
  165.5 0.0 collective-permute-done.below
  165.5 0.0 collective-permute-done.1.above
  165.5 0.0 copy-done.2
  165.5 0.0 copy-start.4
  165.5 0.9 copy-done.4
  166.4 6.7 %correct.1 = f32[3,4,64,1024]{3,2,1,0:T(8,128)} custom-call(f32[4]{0:T(128)S(1)} %add_convert_fusion.flags, f32[3,4,64,1024]{3,2,1,0:T(8,128)} %copy-done.1, f32[4,64,1024]{2,1,0:T(8,128)S(1)} %get-tuple-element.15.partial, f32[3,64,1024]{2,1,0:T(8,128)S(1)} %collective-permute-done.below, f32[3,64,1024]{2,1,0:T(8,128)} %collective-permute-done.1.above, ...), custom_call_target="tpu_custom_call" | custom-call | tf_op jit(solution)/shard_map/correct/pallas_call | solution.py:338
Async XLA Ops:
  0.7 1.9 %copy-start = (f32[1,1024,3,256]{3,1,2,0:T(8,128)S(1)}, f32[1,1024,3,256]{3,1,2,0:T(8,128)}, u32[]{:S(2)}) copy-start(f32[1,1024,3,256]{3,1,2,0:T(8,128)} %param.6) | copy-start | bytes 9437188
  2.6 0.7 copy-start.5
  3.3 0.7 copy-start.6
  104.4 61.1 %copy-start.2 = (s32[4,64,1024]{2,1,0:T(8,128)S(1)}, s32[4,64,1024]{2,1,0:T(8,128)}, u32[]{:S(2)}) copy-start(s32[4,64,1024]{2,1,0:T(8,128)} %active.1) | copy-start | bytes 3145732
  121.4 1.7 copy-start.1
  123.0 26.7 %copy-start.3 = (f32[5,8,1024]{2,1,0:T(8,128)}, f32[5,8,1024]{2,1,0:T(8,128)S(1)}, u32[]{:S(2)}) copy-start(f32[5,8,1024]{2,1,0:T(8,128)S(1)} %get-tuple-element.19.own) | copy-start | bytes 491524
  123.0 42.5 %collective-permute-start = (f32[3,64,1024]{2,1,0:T(8,128)}, f32[3,64,1024]{2,1,0:T(8,128)S(1)}, u32[]{:S(2)}, u32[]{:S(2)}) collective-permute-start(f32[3,64,1024]{2,1,0:T(8,128)} %get-tuple-element.16), channel_id=1, source_target_pairs={{0,4},{4,8},{8,12},{12,16},{16,20},{20,24},{24,28},{28,32},{32,36}... | collective-permute-start | bytes 2359304 | tf_op jit(solution)/shard_map/ppermute | solution.py:352
  126.9 38.6 %collective-permute-start.1 = (f32[3,64,1024]{2,1,0:T(8,128)}, f32[3,64,1024]{2,1,0:T(8,128)}, u32[]{:S(2)}, u32[]{:S(2)}) collective-permute-start(f32[3,64,1024]{2,1,0:T(8,128)} %get-tuple-element.17), channel_id=1, source_target_pairs={{4,0},{8,4},{12,8},{16,12},{20,16},{24,20},{28,24},{32,28},{36,32}... | collective-permute-start | bytes 2359304 | tf_op jit(solution)/shard_map/ppermute | solution.py:352
  132.8 16.0 %collective-permute-start.2 = (f32[5,8,1024]{2,1,0:T(8,128)S(1)}, f32[5,8,1024]{2,1,0:T(8,128)S(1)}, u32[]{:S(2)}, u32[]{:S(2)}) collective-permute-start(f32[5,8,1024]{2,1,0:T(8,128)S(1)} %get-tuple-element.18), channel_id=1, source_target_pairs={{0,1},{1,2},{2,3},{4,5},{5,6},{6,7},{8,9},{9,10},{10,11},{12,13},{... | collective-permute-start | bytes 491528 | tf_op jit(solution)/shard_map/ppermute | solution.py:352
  139.9 9.8 %collective-permute-start.3 = (f32[5,8,1024]{2,1,0:T(8,128)S(1)}, f32[5,8,1024]{2,1,0:T(8,128)S(1)}, u32[]{:S(2)}, u32[]{:S(2)}) collective-permute-start(f32[5,8,1024]{2,1,0:T(8,128)S(1)} %get-tuple-element.19.own), channel_id=1, source_target_pairs={{1,0},{2,1},{3,2},{5,4},{6,5},{7,6},{9,8},{10,9},{11,10},{13,12},{... | collective-permute-start | bytes 491528 | tf_op jit(solution)/shard_map/ppermute | solution.py:352
  148.8 0.8 copy-start.7
  149.7 0.7 copy-start.8
  152.2 11.6 %collective-permute-start.4 = (f32[3,8,1024]{2,1,0:T(8,128)}, f32[3,8,1024]{2,1,0:T(8,128)S(1)}, u32[]{:S(2)}, u32[]{:S(2)}) collective-permute-start(f32[3,8,1024]{2,1,0:T(8,128)} %get-tuple-element.21), channel_id=1, source_target_pairs={{0,4},{4,8},{8,12},{12,16},{16,20},{20,24},{24,28},{28,32},{32,36}... | collective-permute-start | bytes 294920 | tf_op jit(solution)/shard_map/ppermute | solution.py:352
  154.1 11.4 %collective-permute-start.5 = (f32[3,8,1024]{2,1,0:T(8,128)}, f32[3,8,1024]{2,1,0:T(8,128)S(1)}, u32[]{:S(2)}, u32[]{:S(2)}) collective-permute-start(f32[3,8,1024]{2,1,0:T(8,128)} %get-tuple-element.22), channel_id=1, source_target_pairs={{4,0},{8,4},{12,8},{16,12},{20,16},{24,20},{28,24},{32,28},{36,32}... | collective-permute-start | bytes 294920 | tf_op jit(solution)/shard_map/ppermute | solution.py:352
  165.5 0.9 copy-start.4
